TPU v7x, 32 devices: a whole 2x2x4 slice. The times are simulated.
32 devices in a mesh: ctx: 8 (over y, x, core), head: 4 (over z).
Axes of the slice: x: 2, y: 2, z: 4, core: 2. Of those that a mesh axis runs over, the one named last changes fastest.
Arguments:
- prompt_values: bfloat16 [4096, 8192], P('ctx', 'head'), may hold values from -6 to 6
- prompt_gate: bfloat16 [4096, 8192], P('ctx', 'head'), may hold values from -6 to 6
- prompt_inject: bfloat16 [4096, 4, 256], P('ctx', 'head'), may hold values from -6 to 6
- prompt_read: bfloat16 [4096, 4, 256], P('ctx', 'head'), may hold values from -0.375 to 0.375
- prompt_step: float32 [128, 4096], P('head', 'ctx'), may hold values from -8 to 256
- decay_log: float32 [128], P('head'), may hold values from -10 to 0
- skip_gain: float32 [128], P('head'), may hold values from 0.5 to 1.5
- norm_weight: float32 [8192], P('head'), may hold values from 0.1 to 1.9
- out_weight: bfloat16 [8192, 4096], P('head'), may hold values from -0.0625 to 0.0625
- sample_values: bfloat16 [16, 16, 8192], P('ctx', None, 'head'), may hold values from -6 to 6
- sample_gate: bfloat16 [16, 16, 8192], P('ctx', None, 'head'), may hold values from -6 to 6
- sample_inject: bfloat16 [16, 16, 4, 256], P('ctx', None, 'head'), may hold values from -6 to 6
- sample_read: bfloat16 [16, 16, 4, 256], P('ctx', None, 'head'), may hold values from -0.375 to 0.375
- sample_step: float32 [128, 16, 16], P('head', 'ctx'), may hold values from -8 to 256
- sample_length: int32 [16], P('ctx'), may hold values from 1 to 16
Outputs:
- prompt_mixed: bfloat16 [4096, 4096], P('head', 'ctx')
- sample_mixed: bfloat16 [4096, 16], P('head', 'ctx')
All inputs are finite; a program needn't handle non-finite values.
Results may differ from a plain program's by a relative error of at most 0.02.
Values may be sent and summed in bfloat16 or wider, within the bound.
A program may use at most 192 MiB of HBM per device.

v0:
```python
import jax
import jax.numpy as jnp
from jax import lax
from jax.sharding import PartitionSpec as P

HEAD_DIM = 64
STATE = 256
BLOCK = 128
SLEN = 16


full_precision = lax.Precision.HIGHEST


def entering(shard, axis, combine, identity):
    peers, place = (lax.axis_size(axis), lax.axis_index(axis))
    everything = jax.tree.map(
        lambda part, kind: lax.all_gather(part.astype(kind), axis),
        shard,
        (jnp.bfloat16, jnp.bfloat16),
    )
    start = jax.tree.map(
        lambda part, zero: jnp.broadcast_to(jnp.asarray(zero, part.dtype), part.shape),
        shard,
        identity,
    )

    def entering_turn(k, before):
        reached = k < place
        new = combine(
            before, jax.tree.map(lambda part, own: part[k].astype(own.dtype), everything, shard)
        )
        return jax.tree.map(lambda a, b: jnp.where(reached, a, b), new, before)

    return lax.fori_loop(0, peers, entering_turn, start)


def prefix(shard, axis, combine, identity):
    peers, place = (lax.axis_size(axis), lax.axis_index(axis))
    everything = lax.all_gather(shard, axis)
    start = jnp.broadcast_to(jnp.asarray(identity, shard.dtype), shard.shape)

    def prefix_turn(k, before):
        at = peers - 1 - k
        reached = at > place
        new = combine(before, everything[at])
        return jnp.where(reached, new, before)

    return lax.fori_loop(0, peers, prefix_turn, start)


def block_terms(values, inject, readout, steps, decay_rate):
    length = values.shape[0]
    log_decay = steps * decay_rate[:, None]
    running = jnp.cumsum(log_decay, axis=1)
    scores = jnp.dot(
        readout.astype(jnp.float32), inject.astype(jnp.float32).T, precision=full_precision
    )
    causal = jnp.arange(length)[:, None] >= jnp.arange(length)[None, :]
    gap_logs = jnp.where(causal[None], running[:, :, None] - running[:, None, :], 0.0)
    mixing = jnp.where(
        causal[None], scores[None] * jnp.exp(gap_logs) * steps[:, None, :], 0.0
    ).astype(jnp.bfloat16)
    local_out = jnp.einsum(
        "hts,shp->thp",
        mixing.astype(jnp.float32),
        values.astype(jnp.float32),
        precision=full_precision,
    )
    to_end = jnp.exp(running[:, -1:] - running) * steps
    weighted = (to_end[:, :, None] * inject.astype(jnp.float32)[None]).astype(jnp.bfloat16)
    local_state = jnp.einsum(
        "shp,hsn->hpn",
        values.astype(jnp.float32),
        weighted.astype(jnp.float32),
        precision=full_precision,
    )
    return (local_out, local_state, running)


def group_block(values, inject, readout, steps, decay_rate, carry_state):
    local_out, local_state, running = block_terms(values, inject, readout, steps, decay_rate)
    carried = jnp.einsum(
        "tn,hpn->thp", readout.astype(jnp.float32), carry_state, precision=full_precision
    )
    carried = carried * jnp.exp(running).T[:, :, None]
    next_state = jnp.exp(running[:, -1])[:, None, None] * carry_state + local_state
    return (local_out + carried, next_state, running)


def finish(outputs, values, gate, skip_gain, norm_weight, groups):
    row_count = values.shape[0]
    with_skip = outputs + skip_gain[None, :, None] * values.reshape(
        row_count, skip_gain.shape[0], -1
    ).astype(jnp.float32)
    gated_out = with_skip.reshape(row_count, -1) * jax.nn.silu(gate.astype(jnp.float32))
    grouped = gated_out.reshape(row_count, groups, -1)
    inverse_rms = lax.rsqrt(jnp.mean(grouped * grouped, axis=2, keepdims=True) + 1e-05)
    return ((grouped * inverse_rms).reshape(row_count, -1) * norm_weight[None]).astype(jnp.bfloat16)


def chain_pair(before_pair, after_pair):
    return (
        before_pair[0] + after_pair[0],
        jnp.exp(after_pair[0])[:, :, None, None] * before_pair[1] + after_pair[1],
    )


def add_logs(before_logs, after_logs):
    return before_logs + after_logs


def projector(out_weight, row_matrix):
    return lax.dot_general(
        out_weight.astype(jnp.float32),
        row_matrix.astype(jnp.float32),
        (((0,), (1,)), ((), ())),
        precision=full_precision,
    )


def per_device(
    prompt_values,
    prompt_gate,
    prompt_inject,
    prompt_read,
    prompt_step,
    decay_log,
    skip_gain,
    norm_weight,
    out_weight,
    sample_values,
    sample_gate,
    sample_inject,
    sample_read,
    sample_step,
    sample_length,
):
    tokens = prompt_values.shape[0]
    local_groups = prompt_inject.shape[1]
    local_heads = prompt_step.shape[0]
    per_group = local_heads // local_groups
    blocks = tokens // BLOCK
    samples = sample_values.shape[0]
    decay_rate = (-jnp.exp(decay_log)).reshape(local_groups, per_group)
    steps = (
        jax.nn.softplus(prompt_step)
        .reshape(local_groups, per_group, blocks, BLOCK)
        .transpose(2, 0, 1, 3)
    )
    values = prompt_values.reshape(blocks, BLOCK, local_groups, per_group, HEAD_DIM)
    inject = prompt_inject.reshape(blocks, BLOCK, local_groups, STATE)
    readout = prompt_read.reshape(blocks, BLOCK, local_groups, STATE)
    grouped_block = jax.vmap(group_block, in_axes=(1, 1, 1, 0, 0, 0), out_axes=(1, 0, 0))

    def advance(carried_pair, block_data):
        carry_state, offset = carried_pair
        block_values, block_inject, block_readout, block_steps = block_data
        block_out, next_state, running = grouped_block(
            block_values, block_inject, block_readout, block_steps, decay_rate, carry_state
        )
        return ((next_state, offset + running[:, :, -1]), (block_out, running + offset[:, :, None]))

    zero_state = jnp.zeros((local_groups, per_group, HEAD_DIM, STATE), jnp.float32)
    zero_log = jnp.zeros((local_groups, per_group), jnp.float32)
    (end_state, total_log), (outputs, prefix_log) = lax.scan(
        advance, (zero_state, zero_log), (values, inject, readout, steps)
    )
    incoming_log, incoming_state = entering(
        (total_log, end_state), "ctx", chain_pair, (zero_log, zero_state)
    )
    arrival = jnp.einsum(
        "tgn,ghpn->tghp", prompt_read.astype(jnp.float32), incoming_state, precision=full_precision
    )
    decay_in = jnp.exp(prefix_log).transpose(0, 3, 1, 2).reshape(tokens, local_groups, per_group)
    outputs = (
        outputs.reshape(tokens, local_groups, per_group, HEAD_DIM)
        + arrival * decay_in[:, :, :, None]
    )
    normed = finish(
        outputs.reshape(tokens, local_heads, HEAD_DIM),
        prompt_values,
        prompt_gate,
        skip_gain,
        norm_weight,
        local_groups,
    )
    sample_steps = (
        jax.nn.softplus(sample_step)
        .reshape(local_groups, per_group, samples, SLEN)
        .transpose(2, 0, 1, 3)
    )
    sample_vals = sample_values.reshape(samples, SLEN, local_groups, per_group, HEAD_DIM)
    per_sample = jax.vmap(grouped_block, in_axes=(0, 0, 0, 0, None, None), out_axes=(0, 0, 0))
    onehot = (jnp.arange(SLEN)[None, :] == (sample_length - 1)[:, None]).astype(jnp.float32)
    tail_log = prefix(total_log, "ctx", add_logs, zero_log)
    decayed = jnp.exp(tail_log)[:, :, None, None] * end_state
    last_read = jnp.einsum("sl,slgn->sgn", onehot, sample_read.astype(jnp.float32)).astype(
        jnp.bfloat16
    )
    all_read = lax.all_gather(last_read, "ctx", axis=0, tiled=True)
    readings = jnp.einsum(
        "sgn,ghpn->sghp", all_read.astype(jnp.float32), decayed, precision=full_precision
    )
    arriving = lax.psum_scatter(
        readings.astype(jnp.bfloat16), "ctx", scatter_dimension=0, tiled=True
    ).astype(jnp.float32)
    local_out, unused_state, sample_running = per_sample(
        sample_vals, sample_inject, sample_read, sample_steps, decay_rate, zero_state
    )
    local_pick = jnp.einsum("sl,slghp->sghp", onehot, local_out)
    running_pick = jnp.einsum("sl,sghl->sgh", onehot, sample_running)
    joined_out = local_pick + arriving * jnp.exp(running_pick)[:, :, :, None]
    picked_vals = jnp.einsum("sl,slc->sc", onehot, sample_values.astype(jnp.float32)).astype(
        jnp.bfloat16
    )
    picked_gate = jnp.einsum("sl,slc->sc", onehot, sample_gate.astype(jnp.float32)).astype(
        jnp.bfloat16
    )
    picked = finish(
        joined_out.reshape(samples, local_heads, HEAD_DIM),
        picked_vals,
        picked_gate,
        skip_gain,
        norm_weight,
        local_groups,
    )
    prompt_mixed = lax.psum_scatter(
        projector(out_weight, normed).astype(jnp.bfloat16), "head", scatter_dimension=0, tiled=True
    )
    sample_mixed = lax.psum_scatter(
        projector(out_weight, picked).astype(jnp.bfloat16), "head", scatter_dimension=0, tiled=True
    )
    return (prompt_mixed, sample_mixed)


def solution(mesh):
    in_specs = (
        P("ctx", "head"),
        P("ctx", "head"),
        P("ctx", "head", None),
        P("ctx", "head", None),
        P("head", "ctx"),
        P("head"),
        P("head"),
        P("head"),
        P("head", None),
        P("ctx", None, "head"),
        P("ctx", None, "head"),
        P("ctx", None, "head", None),
        P("ctx", None, "head", None),
        P("head", "ctx", None),
        P("ctx"),
    )
    out_specs = (P("head", "ctx"), P("head", "ctx"))
    return jax.shard_map(
        per_device, mesh=mesh, in_specs=in_specs, out_specs=out_specs, check_vma=False
    )
```

profile of v0, /device:TPU:10, one launch (start us, length us, event | category | flops | bytes accessed | tf_op | source)
XLA Modules:
  0.0 405.3 jit_solution(4047086981066365831)
XLA Ops:
  7.3 0.7 exponential_negate_fusion
  7.9 7.1 %reshape.441 = bf16[4,128,1,32,64]{4,3,1,0,2:T(8,128)(2,1)} reshape(bf16[512,2048]{1,0:T(8,128)(2,1)} %param.21) | data formatting | bytes 4194304 | tf_op jit(solution)/shard_map/reshape | solution.py:151
  15.0 6.5 %copy.38 = bf16[4,128,1,32,64]{1,4,3,2,0:T(8,128)(2,1)} copy(bf16[4,128,1,32,64]{4,3,1,0,2:T(8,128)(2,1)} %reshape.441) | data formatting | bytes 4194304
  21.6 138.4 %while.47 = (s32[]{:T(128)}, f32[1,32,64,256]{3,2,1,0:T(8,128)S(1)}, f32[1,32]{1,0:T(1,128)S(1)}, f32[4,128,1,32,64]{1,0,4,3,2:T(4,128)}, f32[4,1,32,128]{3,2,1,...) while((s32[]{:T(128)}, ...), condition=%wide.region_2.3_spmd.clone, body=%wide.region_0.2_spmd.clone.sunk | while | flops 1023471680 | bytes 14618693 | solution.py:166
  21.8 0.3 reduce_window_sum.31
  22.1 1.2 fusion.132
  23.2 1.0 fusion.133
  24.3 2.1 fusion.134
  26.3 26.4 %dynamic_update_slice.14 = f32[4,128,1,32,64]{1,0,4,3,2:T(4,128)} dynamic-update-slice(f32[4,128,1,32,64]{1,0,4,3,2:T(4,128)} %get-tuple-element.547, f32[1,128,1,32,64]{1,0,4,3,2:T(1,128)S(1)} %bitcast.255, s32[]{:T(128)} %get-tuple-element.544, s32[]{:T(128)} %constant.114.clone.1..sunk, s32[]{:T(128)} %constant.114.clone.1..sunk, s32[]{:T(128)} %constant.114.clone.1..sunk, ...) | dynamic-update-slice | bytes 2097156 | tf_op jit(solution)/shard_map/while/body/jit(dynamic_update_index_in_dim)/dynamic_update_slice | solution.py:166
  53.0 0.9 bitcast_convert_fusion.5
  53.9 2.2 bitcast_add_fusion.4
  56.3 0.3 reduce_window_sum.31
  56.7 1.2 fusion.132
  57.8 1.0 fusion.133
  58.8 2.1 fusion.134
  60.9 26.4 %dynamic_update_slice.14 = f32[4,128,1,32,64]{1,0,4,3,2:T(4,128)} dynamic-update-slice(f32[4,128,1,32,64]{1,0,4,3,2:T(4,128)} %get-tuple-element.547, f32[1,128,1,32,64]{1,0,4,3,2:T(1,128)S(1)} %bitcast.255, s32[]{:T(128)} %get-tuple-element.544, s32[]{:T(128)} %constant.114.clone.1..sunk, s32[]{:T(128)} %constant.114.clone.1..sunk, s32[]{:T(128)} %constant.114.clone.1..sunk, ...) | dynamic-update-slice | bytes 2097156 | tf_op jit(solution)/shard_map/while/body/jit(dynamic_update_index_in_dim)/dynamic_update_slice | solution.py:166
  87.6 0.9 bitcast_convert_fusion.5
  88.5 2.2 bitcast_add_fusion.4
  90.9 0.3 reduce_window_sum.31
  91.2 1.2 fusion.132
  92.4 1.0 fusion.133
  93.4 2.1 fusion.134
  95.5 26.4 %dynamic_update_slice.14 = f32[4,128,1,32,64]{1,0,4,3,2:T(4,128)} dynamic-update-slice(f32[4,128,1,32,64]{1,0,4,3,2:T(4,128)} %get-tuple-element.547, f32[1,128,1,32,64]{1,0,4,3,2:T(1,128)S(1)} %bitcast.255, s32[]{:T(128)} %get-tuple-element.544, s32[]{:T(128)} %constant.114.clone.1..sunk, s32[]{:T(128)} %constant.114.clone.1..sunk, s32[]{:T(128)} %constant.114.clone.1..sunk, ...) | dynamic-update-slice | bytes 2097156 | tf_op jit(solution)/shard_map/while/body/jit(dynamic_update_index_in_dim)/dynamic_update_slice | solution.py:166
  122.2 0.9 bitcast_convert_fusion.5
  123.1 2.2 bitcast_add_fusion.4
  125.5 0.3 reduce_window_sum.31
  125.8 1.2 fusion.132
  127.0 1.0 fusion.133
  128.0 2.1 fusion.134
  130.1 26.4 %dynamic_update_slice.14 = f32[4,128,1,32,64]{1,0,4,3,2:T(4,128)} dynamic-update-slice(f32[4,128,1,32,64]{1,0,4,3,2:T(4,128)} %get-tuple-element.547, f32[1,128,1,32,64]{1,0,4,3,2:T(1,128)S(1)} %bitcast.255, s32[]{:T(128)} %get-tuple-element.544, s32[]{:T(128)} %constant.114.clone.1..sunk, s32[]{:T(128)} %constant.114.clone.1..sunk, s32[]{:T(128)} %constant.114.clone.1..sunk, ...) | dynamic-update-slice | bytes 2097156 | tf_op jit(solution)/shard_map/while/body/jit(dynamic_update_index_in_dim)/dynamic_update_slice | solution.py:166
  156.8 0.9 bitcast_convert_fusion.5
  157.7 2.2 bitcast_add_fusion.4
  160.0 8.8 %all-gather.5 = f32[8,1,32]{2,1,0:T(1,128)S(1)} all-gather(f32[1,1,32]{2,1,0:T(1,128)S(1)} %bitcast.271), channel_id=4, replica_groups=mesh['ctx'=8,'head'=4] {'ctx'}, dimensions={0}, use_global_device_ids=true | all-gather | bytes 1152 | tf_op jit(solution)/shard_map/all_gather | solution.py:40
  168.8 0.3 while.49
  169.4 7.9 %all-gather.6 = bf16[8,2,256]{2,1,0:T(2,128)(2,1)S(1)} all-gather(bf16[1,2,256]{2,1,0:T(2,128)(2,1)S(1)} %bitcast.272), channel_id=5, replica_groups=mesh['ctx'=8,'head'=4] {'ctx'}, dimensions={0}, use_global_device_ids=true | all-gather | bytes 9216 | tf_op jit(solution)/shard_map/all_gather | solution.py:201
  177.3 1.5 fusion.61
  178.8 0.7 copy.46
  179.6 1.1 convert_element_type.147
  180.9 0.3 reduce_window_sum.26
  181.9 5.5 %reshape.395 = f32[512,1,32,64]{0,3,2,1:T(8,128)} reshape(f32[4,128,1,32,64]{1,0,4,3,2:T(4,128)} %get-tuple-element.629) | data formatting | bytes 8388608 | tf_op jit(solution)/shard_map/reshape | solution.py:177
  187.5 9.0 %all-gather.4 = bf16[8,1,32]{2,1,0:T(2,128)(2,1)S(1)} all-gather(bf16[1,1,32]{2,1,0:T(2,128)(2,1)S(1)} %convert_bitcast_fusion), channel_id=2, replica_groups=mesh['ctx'=8,'head'=4] {'ctx'}, dimensions={0}, use_global_device_ids=true | all-gather | bytes 576 | tf_op jit(solution)/shard_map/all_gather | solution.py:18
  196.5 0.3 fusion.55
  197.0 0.4 fusion.57
  197.8 16.5 %reduce-scatter.8.cloned.1.call-done = bf16[2,1,32,64]{3,2,1,0:T(8,128)(2,1)} async-done(((bf16[16,1,32,64]{3,2,1,0:T(8,128)(2,1)}), bf16[2,1,32,64]{3,2,1,0:T(8,128)(2,1)}) %reduce-scatter.8.cloned.1.call-update) | async-done | bytes 8208 | tf_op jit(solution)/shard_map/reduce_scatter | solution.py:205
  214.3 0.8 multiply_add_fusion
  215.4 8.1 %fusion.42 = bf16[4096,2]{0,1:T(2,128)(2,1)S(1)} fusion(bf16[2048,4096]{1,0:T(8,128)(2,1)} %param.29, f32[2,2048]{1,0:T(2,128)S(1)} %get-tuple-element.403, f32[2]{0:T(128)S(1)} %add_rsqrt_fusion.1, f32[2048]{0:T(1024)S(1)} %copy-done.7), kind=kOutput, calls=%fused_computation.60 | convolution fusion | flops 33574912 | bytes 16818184 | tf_op jit(solution)/shard_map/dot_general | solution.py:114
  223.5 1.4 copy.58
  225.0 46.1 %all-gather.9.cloned.1.call-done = bf16[8,32,64,256]{3,2,1,0:T(8,128)(2,1)} async-done(((bf16[1,32,64,256]{3,2,1,0:T(8,128)(2,1)}), bf16[8,32,64,256]{3,2,1,0:T(8,128)(2,1)}) %all-gather.9.cloned.1.call-update) | async-done | bytes 8388624 | tf_op jit(solution)/shard_map/all_gather | solution.py:18
  271.1 18.1 %while.48 = (s32[]{:T(128)}, f32[1,32,64,256]{3,2,1,0:T(8,128)S(1)}, s32[]{:T(128)}, bf16[8,1,32]{2,1,0:T(2,128)(2,1)S(1)}, bf16[8,1,32,64,256]{4,3,2,1,0:T(8,128)(2,1)}, /*index=5*/s32[]{:T(128)}, s32[]{:T(128)}) while((s32[]{:T(128)}, f32[1,32,64,256]{3,2,1,0:T(8,128)S(1)}, s32[]{:T(128)}, bf16[8,1,32]{2,1,0:T(2,128)(2,1)S(1)}, ...), condition=%wide.region_4.5_spmd.clone, body=%wide.region_3.4_spmd.clone.sunk | while | flops 2621476 | bytes 5243305 | solution.py:35
  271.1 2.2 fusion.136
  273.3 2.2 fusion.136
  275.6 2.2 fusion.136
  277.9 2.2 fusion.136
  280.1 2.2 fusion.136
  282.4 2.2 fusion.136
  284.7 2.2 fusion.136
  287.0 2.2 fusion.136
  289.2 6.1 %fusion.47 = f32[512,1,32,64]{0,3,2,1:T(8,128)} fusion(f32[512,1,32,64]{0,3,2,1:T(8,128)} %reshape.395, f32[1,32,64,256]{3,2,1,0:T(8,128)S(1)} %get-tuple-element.264, f32[512,32]{0,1:T(8,128)S(1)} %bitcast.268, bf16[512,1,256]{2,0,1:T(8,128)(2,1)S(1)} %bitcast.264), kind=kOutput, calls=%fused_computation.66 | convolution fusion | flops 3223322624 | bytes 10813440 | tf_op jit(solution)/shard_map/tgn,ghpn->tghp/dot_general | solution.py:172
  295.3 5.6 %copy.42 = f32[512,2048]{1,0:T(8,128)} copy(f32[512,2048]{0,1:T(8,128)} %bitcast.256) | data formatting | bytes 8388608 | tf_op jit(solution)/shard_map/reshape | solution.py:181
  300.9 4.5 %multiply_reduce_fusion = (f32[512]{0:T(512)S(1)}, f32[512,2048]{1,0:T(8,128)S(1)}) fusion(bf16[512,2048]{1,0:T(8,128)(2,1)} %param.22, f32[512,2048]{1,0:T(8,128)} %copy.42, bf16[512,2048]{1,0:T(8,128)(2,1)S(1)} %copy-done.2, f32[2048]{0:T(1024)S(1)} %mul.259), kind=kLoop, calls=%fused_computation.68 | loop fusion | flops 11533824 | bytes 12593152 | tf_op jit(solution)/shard_map/reduce_sum | solution.py:98
  305.5 14.1 %fusion.41 = bf16[4096,512]{0,1:T(8,128)(2,1)} fusion(bf16[2048,4096]{1,0:T(8,128)(2,1)} %param.29, f32[512,2048]{1,0:T(8,128)S(1)} %get-tuple-element.405, f32[2048]{0:T(1024)S(1)} %copy-done.7, f32[512]{0:T(512)S(1)} %add_rsqrt_fusion), kind=kOutput, calls=%fused_computation.56 | convolution fusion | flops 8595177472 | bytes 25176064 | tf_op jit(solution)/shard_map/dot_general | solution.py:114
  319.6 1.7 copy.59
  321.3 75.2 %reduce-scatter.6.cloned.1.call-done = bf16[1024,512]{0,1:T(8,128)(2,1)} async-done(((bf16[4096,512]{0,1:T(8,128)(2,1)}), bf16[1024,512]{0,1:T(8,128)(2,1)}) %reduce-scatter.6.cloned.1.call-update) | async-done | bytes 1048592 | tf_op jit(solution)/shard_map/reduce_scatter | solution.py:228
  396.5 2.3 copy.47
  (130 shorter events, 4.5 us)
Async XLA Ops:
  7.2 190.3 %copy-start = (bf16[2,16,2048]{2,1,0:T(8,128)(2,1)S(1)}, bf16[2,16,2048]{2,1,0:T(8,128)(2,1)}, u32[]{:S(2)}) copy-start(bf16[2,16,2048]{2,1,0:T(8,128)(2,1)} %param.31) | copy-start | bytes 393220
  7.2 207.1 %reduce-scatter.8.cloned.1.call-start = ((), (), s32[]{:S(2)}) async-start(), calls=%async_computation.4 | async-start | bytes 147456 | tf_op jit(solution)/shard_map/reduce_scatter | solution.py:205
  15.0 6.5 %copy-start.8 = (f32[32,512]{1,0:T(8,128)S(1)}, f32[32,512]{1,0:T(8,128)}, u32[]{:S(2)}) copy-start(f32[32,512]{1,0:T(8,128)} %param.25) | copy-start | bytes 196612
  15.0 6.6 %copy-start.3 = (bf16[512,1,256]{2,0,1:T(8,128)(2,1)S(1)}, bf16[512,1,256]{2,0,1:T(8,128)(2,1)}, u32[]{:S(2)}) copy-start(bf16[512,1,256]{2,0,1:T(8,128)(2,1)} %param.24) | copy-start | bytes 786436
  21.6 147.5 %copy-start.12 = (s32[2]{0:T(128)S(1)}, s32[2]{0:T(128)}, u32[]{:S(2)}) copy-start(s32[2]{0:T(128)} %param.35) | copy-start | bytes 28
  21.6 147.6 %copy-start.6 = (bf16[2,16,1,256]{3,1,2,0:T(8,128)(2,1)S(1)}, bf16[2,16,1,256]{3,1,2,0:T(8,128)(2,1)}, u32[]{:S(2)}) copy-start(bf16[2,16,1,256]{3,1,2,0:T(8,128)(2,1)} %param.33) | copy-start | bytes 49156
  53.9 2.4 copy-start.4
  88.5 2.4 copy-start.4
  123.1 2.4 copy-start.4
  157.7 2.4 copy-start.4
  179.5 1.3 copy-start.9
  179.5 1.7 copy-start.5
  179.5 2.2 copy-start.11
  179.5 91.5 %all-gather.9.cloned.1.call-start = ((), (), s32[]{:S(2)}) async-start(), calls=%async_computation.5 | async-start | bytes 9437184 | tf_op jit(solution)/shard_map/all_gather | solution.py:18
  180.7 138.8 %reduce-scatter.10.cloned.1.call-start = ((), (), s32[]{:S(2)}) async-start(), calls=%async_computation.6 | async-start | bytes 1310720
  181.9 14.9 %copy-start.10 = (bf16[2,16,1,256]{3,1,2,0:T(8,128)(2,1)S(1)}, bf16[2,16,1,256]{3,1,2,0:T(8,128)(2,1)}, u32[]{:S(2)}) copy-start(bf16[2,16,1,256]{3,1,2,0:T(8,128)(2,1)} %param.32) | copy-start | bytes 49156
  187.4 28.0 %copy-start.7 = (f32[2048]{0:T(1024)S(1)}, f32[2048]{0:T(1024)}, u32[]{:S(2)}) copy-start(f32[2048]{0:T(1024)} %param.28) | copy-start | bytes 24580
  224.9 171.6 %reduce-scatter.6.cloned.1.call-start = ((), (), s32[]{:S(2)}) async-start(), calls=%async_computation.3 | async-start | bytes 5242880 | tf_op jit(solution)/shard_map/reduce_scatter | solution.py:228
  295.3 5.6 %copy-start.2 = (bf16[512,2048]{1,0:T(8,128)(2,1)S(1)}, bf16[512,2048]{1,0:T(8,128)(2,1)}, u32[]{:S(2)}) copy-start(bf16[512,2048]{1,0:T(8,128)(2,1)} %param.21) | copy-start | bytes 6291460
  319.5 79.2 %copy-start.1 = (bf16[2,16,2048]{2,1,0:T(8,128)(2,1)S(1)}, bf16[2,16,2048]{2,1,0:T(8,128)(2,1)}, u32[]{:S(2)}) copy-start(bf16[2,16,2048]{2,1,0:T(8,128)(2,1)} %param.31) | copy-start | bytes 393220
Sparse Core Ops, SparseCore 0:
  179.6 34.6 reduce-scatter.7
  216.8 54.2 all-gather.8
  273.4 25.2 reduce-scatter.9
  319.7 76.7 reduce-scatter.5
where the time goes:
time: 411 us; the launch traced here: 405 us
  local copies, waits for them, and re-layouts  138 us (34%)
  waiting for transfers between devices  138 us (34%)
  matrix products  57.1 us (14%)
  other arithmetic  31.5 us (8%)
  blocking collectives  25.7 us (6%)
  between operations  14.1 us (3%)
    dynamic_update_slice x4, local copies, waits for them, and re-layouts, per_device(): lax.scan(advance, (zero_state, zero_log), (values, inject, readout, steps))  106 us
    reduce_scatter x1, waiting for transfers between devices, per_device(): lax.psum_scatter(projector(out_weight, normed).astype(jnp.bfloat16), 'hea...  75.2 us
    all_gather x1, waiting for transfers between devices, entering(): lax.all_gather(part.astype(kind), axis)  46.1 us
    dot_general x2, matrix products, projector(): lax.dot_general(out_weight.astype(jnp.float32), row_matrix.astype(jnp.flo...  22.1 us
    select_n x8, other arithmetic, entering_turn(): return jax.tree.map(lambda a, b: jnp.where(reached, a, b), new, before)  17.8 us
    reduce_scatter x1, waiting for transfers between devices, per_device(): lax.psum_scatter(readings.astype(jnp.bfloat16), 'ctx', scatter_dimension=...  16.5 us
    unnamed x30, local copies, waits for them, and re-layouts  12 us
    dot_general x4, matrix products, block_terms(): jnp.einsum('shp,hsn->hpn', values.astype(jnp.float32), weighted.astype(jn...  8.97 us
  transfers between devices with their start and end apart: 4, of which 3 were waited for; matrix products, arithmetic and copies ran while one was open for 17% of the time, Pallas kernels for 0%

commit v1 on v0

v1 whole, which is shorter than its diff:
```python
import functools

import jax
import jax.numpy as jnp
from jax import lax
from jax.experimental import pallas as pl
from jax.experimental.pallas import tpu as pltpu
from jax.sharding import PartitionSpec as P

BLOCK = 128
LANES = 128
PAD = 8
F32 = jnp.float32
BF16 = jnp.bfloat16
EXACT = lax.Precision.HIGHEST
VMEM_LIMIT = 60 * 1024 * 1024


def dot(a, b, dims=((1,), (0,)), precision=None):
    return lax.dot_general(a, b, (dims, ((), ())), precision=precision, preferred_element_type=F32)


def softplus(v):
    return jnp.maximum(v, 0.0) + jnp.log1p(jnp.exp(-jnp.abs(v)))


def silu(v):
    return v / (1.0 + jnp.exp(-v))


def spread(w, expander):
    high = w.astype(BF16)
    low = (w - high.astype(F32)).astype(BF16)
    return dot(jnp.concatenate([high, low], axis=1), expander)


def expander_of(heads, dim):
    row = lax.broadcasted_iota(jnp.int32, (2 * heads, heads * dim), 0)
    lane = lax.broadcasted_iota(jnp.int32, (2 * heads, heads * dim), 1)
    head = lane // dim
    return jnp.where((row == head) | (row == head + heads), 1.0, 0.0).astype(BF16)


def square(n):
    return (
        lax.broadcasted_iota(jnp.int32, (n, n), 0),
        lax.broadcasted_iota(jnp.int32, (n, n), 1),
    )


def state_kernel(dim, values_ref, inject_ref, step_ref, rate_ref, state_ref, log_ref, scaled_ref):
    tokens, channels = values_ref.shape
    heads = channels // dim
    steps = softplus(step_ref[...])
    logs = steps * rate_ref[...]
    i, j = square(tokens)
    after = dot(jnp.where(j > i, 1.0, 0.0), logs, ((1,), (1,)), EXACT)
    total = dot(jnp.ones((PAD, tokens), F32), logs, ((1,), (1,)), EXACT)
    turned = dot(jnp.where(i == j, 1.0, 0.0), steps, ((1,), (1,)), EXACT)
    weight = jnp.exp(after) * turned
    expander = expander_of(heads, dim)
    for b in range(tokens // BLOCK):
        rows = pl.ds(b * BLOCK, BLOCK)
        wide = spread(weight[b * BLOCK : (b + 1) * BLOCK], expander)
        scaled_ref[rows, :] = (wide * values_ref[rows, :].astype(F32)).astype(BF16)
    state_ref[...] = dot(inject_ref[...], scaled_ref[...], ((0,), (0,))).astype(BF16)
    log_ref[...] = dot(total, expander[:heads].astype(F32), precision=EXACT)


def local_kernel(
    dim,
    values_ref,
    gate_ref,
    inject_ref,
    read_ref,
    step_ref,
    rate_ref,
    skip_ref,
    out_ref,
    gain_ref,
    state_ref,
    offset_ref,
    part_ref,
):
    channels = values_ref.shape[1]
    heads = channels // dim

    @pl.when(pl.program_id(0) == 0)
    def _():
        state_ref[...] = jnp.zeros_like(state_ref)
        offset_ref[...] = jnp.zeros_like(offset_ref)

    steps = softplus(step_ref[...])
    logs = steps * rate_ref[...]
    i, j = square(BLOCK)
    lower = jnp.where(i >= j, 1.0, 0.0)
    running = dot(logs, lower, ((1,), (1,)), EXACT)
    running_t = dot(lower, logs, ((1,), (1,)), EXACT)
    after = dot(jnp.where(j > i, 1.0, 0.0), logs, ((1,), (1,)), EXACT)
    turned = dot(jnp.where(i == j, 1.0, 0.0), steps, ((1,), (1,)), EXACT)
    expander = expander_of(heads, dim)
    inject = inject_ref[...]
    readout = read_ref[...]
    scores = jnp.where(i >= j, dot(readout, inject, ((1,), (1,))), 0.0)
    per = LANES // dim
    lane = lax.broadcasted_iota(jnp.int32, (BLOCK, LANES), 1)
    for k in range(heads // per):
        cols = slice(k * LANES, (k + 1) * LANES)
        pair = values_ref[:, cols]
        mixes, parts = [], []
        for q in range(per):
            h = k * per + q
            gap = jnp.minimum(running_t[:, h : h + 1] - running[h : h + 1, :], 0.0)
            mixes.append((scores * jnp.exp(gap) * steps[h : h + 1, :]).astype(BF16))
            parts.append(jnp.where(lane // dim == q, pair, jnp.zeros_like(pair)))
        part_ref[:, cols] = dot(jnp.concatenate(mixes, axis=1), jnp.concatenate(parts, axis=0))
    decay = spread(jnp.exp(running_t), expander)
    values = values_ref[...].astype(F32)
    opened = silu(gate_ref[...].astype(F32))
    total = part_ref[...] + skip_ref[...] * values
    total = total + dot(readout, state_ref[...].astype(BF16)) * decay
    out_ref[...] = (total * opened).astype(BF16)
    offset = offset_ref[0:1, :]
    gain_ref[...] = (opened * spread(jnp.exp(running_t + offset), expander)).astype(BF16)
    offset_ref[0:1, :] = offset + running_t[BLOCK - 1 : BLOCK, :]
    scaled = (spread(jnp.exp(after) * turned, expander) * values).astype(BF16)
    state_ref[...] = state_ref[...] * decay[BLOCK - 1 : BLOCK, :] + dot(
        inject, scaled, ((0,), (0,))
    )


def sample_kernel(
    dim,
    length_ref,
    values_ref,
    gate_ref,
    inject_ref,
    read_ref,
    step_ref,
    rate_ref,
    skip_ref,
    out_ref,
    gain_ref,
    picked_ref,
):
    samples, length, channels = values_ref.shape
    heads = channels // dim
    out_ref[...] = jnp.zeros_like(out_ref)
    gain_ref[...] = jnp.zeros_like(gain_ref)
    picked_ref[...] = jnp.zeros_like(picked_ref)
    u, s = square(length)
    own = lax.broadcasted_iota(jnp.int32, (heads, channels), 1) // dim == (
        lax.broadcasted_iota(jnp.int32, (heads, channels), 0)
    )
    at = lax.broadcasted_iota(jnp.int32, (1, length), 1)
    for k in range(samples):
        last = length_ref[k] - 1
        hot = jnp.where(lax.broadcasted_iota(jnp.int32, (PAD, length), 1) == last, 1.0, 0.0).astype(BF16)
        steps = softplus(step_ref[k])
        logs = steps * rate_ref[...]
        between = jnp.where((u > s) & (u <= last), 1.0, 0.0)
        gap = dot(logs, between, precision=EXACT)
        running = jnp.sum(jnp.where(at <= last, logs, 0.0), axis=1, keepdims=True)
        row = dot(hot, read_ref[k])
        score = dot(row.astype(BF16), inject_ref[k], ((1,), (1,)))[0:1]
        mixing = jnp.where(at <= last, score * jnp.exp(gap) * steps, 0.0).astype(BF16)
        values = values_ref[k]
        local = jnp.sum(jnp.where(own, dot(mixing, values), 0.0), axis=0, keepdims=True)
        decay = jnp.sum(jnp.where(own, jnp.exp(running), 0.0), axis=0, keepdims=True)
        value = dot(hot, values)[0:1]
        opened = silu(dot(hot, gate_ref[k])[0:1])
        out_ref[k : k + 1, :] = (local + skip_ref[...] * value) * opened
        gain_ref[k : k + 1, :] = decay * opened
        picked_ref[k : k + 1, :] = row[0:1]


def finish_rows(total, weight):
    mean = jnp.mean(total * total, axis=1, keepdims=True)
    return (total * lax.rsqrt(mean + 1e-05) * weight).astype(BF16)


def finish_kernel(
    read_ref,
    state_ref,
    out_ref,
    gain_ref,
    picked_ref,
    final_ref,
    sample_out_ref,
    sample_gain_ref,
    weight_ref,
    normed_ref,
):
    tokens = read_ref.shape[0]
    for b in range(tokens // BLOCK):
        rows = pl.ds(b * BLOCK, BLOCK)
        arrival = dot(read_ref[rows, :], state_ref[...])
        total = out_ref[rows, :].astype(F32) + arrival * gain_ref[rows, :].astype(F32)
        normed_ref[rows, :] = finish_rows(total, weight_ref[...])
    arrival = dot(picked_ref[...].astype(BF16), final_ref[...])
    total = sample_out_ref[...] + arrival * sample_gain_ref[...]
    normed_ref[pl.ds(tokens, total.shape[0]), :] = finish_rows(total, weight_ref[...])


def scan_states(state, logs, axis):
    peers, place = (lax.axis_size(axis), lax.axis_index(axis))
    before = jnp.zeros_like(state)
    total = state
    stride = 1
    while stride < peers:
        pairs = [(p, p ^ stride) for p in range(peers)]
        other = lax.ppermute(total, axis, pairs)
        other_logs = lax.ppermute(logs, axis, pairs)
        upper = (place // stride) % 2 == 1
        own_total, own_logs = total, logs
        first = jnp.where(upper, other, own_total).astype(F32)
        second = jnp.where(upper, own_total, other).astype(F32)
        second_logs = jnp.where(upper, own_logs, other_logs)
        total = (jnp.exp(second_logs) * first + second).astype(BF16)
        if stride == 1:
            before_logs = jnp.zeros_like(logs)
        before = jnp.where(
            upper,
            jnp.exp(before_logs) * other.astype(F32) + before.astype(F32),
            before.astype(F32),
        ).astype(BF16)
        before_logs = jnp.where(upper, before_logs + other_logs, before_logs)
        logs = own_logs + other_logs
        stride *= 2
    return before, total


def call(body, outs, scratch=(), flops=0, **more):
    return pl.pallas_call(
        body,
        out_shape=outs,
        scratch_shapes=list(scratch),
        compiler_params=pltpu.CompilerParams(vmem_limit_bytes=VMEM_LIMIT),
        cost_estimate=pl.CostEstimate(flops=flops, bytes_accessed=8 << 20, transcendentals=0),
        **more,
    )


def per_device(
    prompt_values,
    prompt_gate,
    prompt_inject,
    prompt_read,
    prompt_step,
    decay_log,
    skip_gain,
    norm_weight,
    out_weight,
    sample_values,
    sample_gate,
    sample_inject,
    sample_read,
    sample_step,
    sample_length,
):
    tokens, channels = prompt_values.shape
    heads = prompt_step.shape[0]
    dim = channels // heads
    entries = prompt_inject.shape[2]
    samples, length = sample_values.shape[:2]
    inject = prompt_inject.reshape(tokens, entries)
    readout = prompt_read.reshape(tokens, entries)
    rate = -jnp.exp(decay_log)[:, None]
    skip = jnp.repeat(skip_gain, dim)[None]
    weight = norm_weight[None]
    shape = jax.ShapeDtypeStruct

    state, logs = call(
        functools.partial(state_kernel, dim),
        (shape((entries, channels), BF16), shape((PAD, channels), F32)),
        [pltpu.VMEM((tokens, channels), BF16)],
        flops=2 << 30,
    )(prompt_values, inject, prompt_step, rate)

    def block(width):
        return pl.BlockSpec((BLOCK, width), lambda b: (b, 0))

    def whole(*sizes):
        return pl.BlockSpec(sizes, lambda b: (0,) * len(sizes))

    out, gain = call(
        functools.partial(local_kernel, dim),
        (shape((tokens, channels), BF16), shape((tokens, channels), BF16)),
        [
            pltpu.VMEM((entries, channels), F32),
            pltpu.VMEM((PAD, heads), F32),
            pltpu.VMEM((BLOCK, channels), F32),
        ],
        flops=8 << 30,
        grid=(tokens // BLOCK,),
        in_specs=[
            block(channels),
            block(channels),
            block(entries),
            block(entries),
            pl.BlockSpec((heads, BLOCK), lambda b: (0, b)),
            whole(heads, 1),
            whole(1, channels),
        ],
        out_specs=(block(channels), block(channels)),
    )(prompt_values, prompt_gate, inject, readout, prompt_step, rate, skip)
    padded = -(-samples // PAD) * PAD
    vmem = pl.BlockSpec(memory_space=pltpu.VMEM)
    sample_out, sample_gain, picked = call(
        functools.partial(sample_kernel, dim),
        (
            shape((padded, channels), F32),
            shape((padded, channels), F32),
            shape((padded, entries), F32),
        ),
        flops=4 << 30,
        in_specs=[pl.BlockSpec(memory_space=pltpu.SMEM)] + [vmem] * 7,
    )(
        sample_length,
        sample_values,
        sample_gate,
        sample_inject.reshape(samples, length, entries),
        sample_read.reshape(samples, length, entries),
        sample_step.transpose(1, 0, 2),
        rate,
        skip,
    )
    before, final = scan_states(state, logs[:1], "ctx")
    normed = call(finish_kernel, shape((tokens + padded, channels), BF16), flops=1 << 30)(
        readout, before, out, gain, picked, final, sample_out, sample_gain, weight
    )
    return project(normed, out_weight, tokens, samples)


def project(normed, out_weight, tokens, samples):
    share = dot(normed, out_weight).astype(BF16)
    mixed = lax.psum_scatter(share, "head", scatter_dimension=1, tiled=True)
    return mixed[:tokens].T, mixed[tokens : tokens + samples].T


def solution(mesh):
    in_specs = (
        P("ctx", "head"),
        P("ctx", "head"),
        P("ctx", "head", None),
        P("ctx", "head", None),
        P("head", "ctx"),
        P("head"),
        P("head"),
        P("head"),
        P("head", None),
        P("ctx", None, "head"),
        P("ctx", None, "head"),
        P("ctx", None, "head", None),
        P("ctx", None, "head", None),
        P("head", "ctx", None),
        P("ctx"),
    )
    out_specs = (P("head", "ctx"), P("head", "ctx"))
    return jax.shard_map(
        per_device, mesh=mesh, in_specs=in_specs, out_specs=out_specs, check_vma=False
    )
```

time: 411 us -> 188 us (0.46)
  local copies, waits for them, and re-layouts: 138 us -> 6.92 us
  matrix products: 57.1 us -> 14.6 us
  waiting for transfers between devices: 138 us -> 110 us
  Pallas kernels: 0 us -> 27 us
  blocking collectives: 25.7 us -> 0 us
  other arithmetic: 31.5 us -> 8.34 us
  starting transfers between devices: 0.16 us -> 4.65 us
    dynamic_update_slice x4 -> x0, local copies, waits for them, and re-layouts: 106 us -> none  [per_device(): lax.scan(advance, (zero_state, zero_log), (values, inject, readout, steps))]
    all_gather x1 -> x0, waiting for transfers between devices: 46.1 us -> none  [entering(): lax.all_gather(part.astype(kind), axis)]
    dot_general x28 -> x1, matrix products: 57.1 us -> 14.6 us  [dot(): lax.dot_general(a, b, (dims, ((), ())), precision=precision, preferred_el...]
    ppermute x0 -> x6, waiting for transfers between devices: none -> 31.2 us  [the longest x3 31.2 us: scan_states(): other_logs = lax.ppermute(logs, axis, pairs)]
    pallas_call x0 -> x4, Pallas kernels: none -> 27 us  [the longest x1 12.4 us: per_device(): call(functools.partial(local_kernel, dim), (shape((tokens, channels), BF1...]
    all_gather x3 -> x0, blocking collectives: 25.7 us -> none  [the longest x1 8.96 us: entering(): lax.all_gather(part.astype(kind), axis)]
    reshape x5 -> x0, local copies, waits for them, and re-layouts: 18.3 us -> none  [the longest x1 7.06 us: per_device(): prompt_values.reshape(blocks, BLOCK, local_groups, per_group, HEAD_DIM)]
    select_n x17 -> x0, other arithmetic: 18 us -> none  [the longest x8 17.8 us: entering_turn(): return jax.tree.map(lambda a, b: jnp.where(reached, a, b), new, before)]
  transfers between devices with their start and end apart: 4 -> 7, of which waited for: 3 -> 4; matrix products, arithmetic and copies ran while one was open for 17% -> 2% of each run, Pallas kernels for 0% -> 8%
where the time goes in v1:
time: 188 us; the launch traced here: 186 us
  waiting for transfers between devices  110 us (59%)
  Pallas kernels  27 us (14%)
  matrix products  14.6 us (8%)
  between operations  14.1 us (8%)
  other arithmetic  8.34 us (4%)
  local copies, waits for them, and re-layouts  6.92 us (4%)
  starting transfers between devices  4.65 us (2%)
    reduce_scatter x1, waiting for transfers between devices, project(): mixed = lax.psum_scatter(share, 'head', scatter_dimension=1, tiled=True)  79.1 us
    ppermute x3, waiting for transfers between devices, scan_states(): other_logs = lax.ppermute(logs, axis, pairs)  31.2 us
    dot_general x1, matrix products, dot(): lax.dot_general(a, b, (dims, ((), ())), precision=precision, preferred_el...  14.6 us
    pallas_call x1, Pallas kernels, per_device(): call(functools.partial(local_kernel, dim), (shape((tokens, channels), BF1...  12.4 us
    convert_element_type x3, other arithmetic, scan_states(): total = (jnp.exp(second_logs) * first + second).astype(BF16)  6.76 us
    pallas_call x1, Pallas kernels, per_device(): call(finish_kernel, shape((tokens + padded, channels), BF16), flops=1 << 30)  6.24 us
    pallas_call x1, Pallas kernels, per_device(): call(functools.partial(state_kernel, dim), (shape((entries, channels), BF...  5.87 us
  transfers between devices with their start and end apart: 7, of which 4 were waited for; matrix products, arithmetic and copies ran while one was open for 2% of the time, Pallas kernels for 8%

profile of v1, /device:TPU:10, one launch (start us, length us, event | category | flops | bytes accessed | tf_op | source)
XLA Modules:
  0.0 186.0 jit_solution(4719821997883487334)
XLA Ops:
  7.2 0.0 reduce-scatter.2.cloned.1.call-start
  7.2 0.7 negate_bitcast_fusion
  7.9 0.7 copy.17.rate_ref
  8.6 5.9 %shard_map.158 = (bf16[256,2048]{1,0:T(8,128)(2,1)}, f32[8,2048]{1,0:T(8,128)}) custom-call(bf16[512,2048]{1,0:T(8,128)(2,1)} %values_ref.4, bf16[512,256]{1,0:T(8,128)(2,1)} %bitcast.28, f32[32,512]{1,0:T(8,128)} %step_ref.3, f32[32,1]{1,0:T(8,128)} %copy.17.rate_ref), custom_call_target="tpu_custom_call" | custom-call | flops 2147483648 | bytes 8388608 | tf_op jit(solution)/shard_map/pallas_call | solution.py:273
  14.4 0.0 copy-start.1
  14.4 0.0 collective-permute-start.2
  14.4 0.9 slice.9
  15.3 0.5 collective-permute-start
  15.8 1.5 collective-permute-done
  17.3 0.9 slice_add_fusion
  18.2 0.0 collective-permute-done.2
  18.2 1.7 add_convert_fusion.2
  19.9 0.6 collective-permute-start.3
  20.5 1.5 collective-permute-start.1
  22.0 0.0 copy-done.1
  22.0 0.1 broadcast_in_dim.15
  22.0 0.7 broadcast_in_dim_reshape.3.skip_ref
  22.7 22.6 %collective-permute-done.1 = f32[1,2048]{1,0:T(1,128)S(1)} collective-permute-done((f32[1,2048]{1,0:T(1,128)S(1)}, f32[1,2048]{1,0:T(1,128)S(1)}, u32[]{:S(2)}, u32[]{:S(2)}) %collective-permute-start.1) | collective-permute-done | bytes 8224 | tf_op jit(solution)/shard_map/ppermute | solution.py:213
  45.4 0.0 collective-permute-done.3
  45.4 1.4 add_convert_fusion.1
  46.8 1.5 collective-permute-start.4
  48.3 0.0 copy-start
  48.3 12.4 %shard_map.159 = (bf16[512,2048]{1,0:T(8,128)(2,1)}, bf16[512,2048]{1,0:T(8,128)(2,1)}) custom-call(bf16[512,2048]{1,0:T(8,128)(2,1)} %values_ref.4, bf16[512,2048]{1,0:T(8,128)(2,1)} %gate_ref.2, bf16[512,256]{1,0:T(8,128)(2,1)} %bitcast.29, bf16[512,256]{1,0:T(8,128)(2,1)} %bitcast.19, f32[32,512]{1,0:T(8,128)} %step_ref.3, f32[32,1]{1,0:T(8,128)} %copy.17.rate_ref, ...), custom_call_target="tpu_custom_call" | custom-call | flops 8589934592 | bytes 8388608 | tf_op jit(solution)/shard_map/pallas_call | solution.py:286
  60.7 0.0 copy-done
  60.7 0.7 copy.19
  61.4 0.5 collective-permute-start.5
  61.9 2.5 %shard_map.160 = (f32[8,2048]{1,0:T(8,128)}, f32[8,2048]{1,0:T(8,128)}, f32[8,256]{1,0:T(8,128)}) custom-call(s32[2]{0:T(128)} %length_ref.1, bf16[2,16,2048]{2,1,0:T(8,128)(2,1)} %values_ref.5, bf16[2,16,2048]{2,1,0:T(8,128)(2,1)} %gate_ref.3, bf16[2,16,256]{2,1,0:T(8,128)(2,1)} %bitcast.30, bf16[2,16,256]{2,1,0:T(8,128)(2,1)} %bitcast.31, ...), custom_call_target="tpu_custom_call" | custom-call | flops 4294967296 | bytes 8388608 | tf_op jit(solution)/shard_map/pallas_call | solution.py:309
  64.4 7.1 %collective-permute-done.5 = f32[1,2048]{1,0:T(1,128)S(1)} collective-permute-done((f32[1,2048]{1,0:T(1,128)S(1)}, f32[1,2048]{1,0:T(1,128)S(1)}, u32[]{:S(2)}, u32[]{:S(2)}) %collective-permute-start.5) | collective-permute-done | bytes 8224 | tf_op jit(solution)/shard_map/ppermute | solution.py:213
  71.5 0.0 collective-permute-done.4
  71.6 3.7 %add_convert_fusion = (bf16[256,2048]{1,0:T(8,128)(2,1)}, bf16[256,2048]{1,0:T(8,128)(2,1)}) fusion(bf16[256,2048]{1,0:T(8,128)(2,1)} %add_convert_fusion.1, bf16[256,2048]{1,0:T(8,128)(2,1)S(1)} %collective-permute-done.4, f32[2048]{0:T(1024)S(1)} %bitcast.23, pred[]{:T(512)S(6)} %eq.13, bf16[256,2048]{1,0:T(8,128)(2,1)S(1)} %collective-permute-done.2, ...), kind=kLoop, calls=%fused_computation.5 | loop fusion | flops 11534336 | bytes 6316035 | tf_op jit(solution)/shard_map/convert_element_type | solution.py:219
  75.2 6.2 %shard_map.161 = bf16[520,2048]{1,0:T(8,128)(2,1)} custom-call(bf16[512,256]{1,0:T(8,128)(2,1)} %bitcast.20, bf16[256,2048]{1,0:T(8,128)(2,1)} %get-tuple-element.19.state_ref, bf16[512,2048]{1,0:T(8,128)(2,1)} %get-tuple-element.11.out_ref, bf16[512,2048]{1,0:T(8,128)(2,1)} %get-tuple-element.12.gain_ref, f32[8,256]{1,0:T(8,128)} %get-tuple-element.13.picked_ref, ...), custom_call_target="tpu_custom_call" | custom-call | flops 1073741824 | bytes 8388608 | tf_op jit(solution)/shard_map/pallas_call | solution.py:329
  81.5 14.6 %convolution_convert_fusion = bf16[520,4096]{1,0:T(8,128)(2,1)} fusion(bf16[520,2048]{1,0:T(8,128)(2,1)} %shard_map.161, bf16[2048,4096]{1,0:T(8,128)(2,1)} %param.23), kind=kOutput, calls=%fused_computation | convolution fusion | flops 8726282240 | bytes 23166976 | tf_op jit(solution)/shard_map/dot_general | solution.py:20
  96.0 0.0 reduce-scatter.2.cloned.1.call-update
  96.1 79.1 %reduce-scatter.2.cloned.1.call-done = bf16[520,1024]{1,0:T(8,128)(2,1)} async-done(((bf16[520,4096]{1,0:T(8,128)(2,1)}), bf16[520,1024]{1,0:T(8,128)(2,1)}) %reduce-scatter.2.cloned.1.call-update) | async-done | bytes 1064976 | tf_op jit(solution)/shard_map/reduce_scatter | solution.py:337
  175.2 1.3 slice_bitcast_fusion
  176.5 1.3 copy.21
  177.8 1.3 slice_bitcast_fusion.1
  (2 shorter events, 0.1 us)
Async XLA Ops:
  7.2 168.0 %reduce-scatter.2.cloned.1.call-start = ((), (), s32[]{:S(2)}) async-start(), calls=%async_computation.1 | async-start | bytes 5324800 | tf_op jit(solution)/shard_map/reduce_scatter | solution.py:337
  14.4 7.5 %copy-start.1 = (f32[32]{0:T(128)S(1)}, f32[32]{0:T(128)}, u32[]{:S(2)}) copy-start(f32[32]{0:T(128)} %param.21) | copy-start | bytes 388
  14.4 3.7 %collective-permute-start.2 = (bf16[256,2048]{1,0:T(8,128)(2,1)}, bf16[256,2048]{1,0:T(8,128)(2,1)S(1)}, u32[]{:S(2)}, u32[]{:S(2)}) collective-permute-start(bf16[256,2048]{1,0:T(8,128)(2,1)} %get-tuple-element.10), channel_id=1, source_target_pairs={{0,4},{4,0},{8,12},{12,8},{16,20},{20,16},{24,28},{28,24},{1,5},{5... | collective-permute-start | bytes 3145736 | tf_op jit(solution)/shard_map/ppermute | solution.py:212
  15.3 2.0 %collective-permute-start = (f32[1,2048]{1,0:T(1,128)S(1)}, f32[1,2048]{1,0:T(1,128)S(1)}, u32[]{:S(2)}, u32[]{:S(2)}) collective-permute-start(f32[1,2048]{1,0:T(1,128)S(1)} %slice.9), channel_id=1, source_target_pairs={{0,4},{4,0},{8,12},{12,8},{16,20},{20,16},{24,28},{28,24},{1,5},{5... | collective-permute-start | bytes 24584 | tf_op jit(solution)/shard_map/ppermute | solution.py:213
  19.9 25.5 %collective-permute-start.3 = (bf16[256,2048]{1,0:T(8,128)(2,1)S(1)}, bf16[256,2048]{1,0:T(8,128)(2,1)S(1)}, u32[]{:S(2)}, u32[]{:S(2)}) collective-permute-start(bf16[256,2048]{1,0:T(8,128)(2,1)S(1)} %add_convert_fusion.2), channel_id=1, source_target_pairs={{0,8},{4,12},{8,0},{12,4},{16,24},{20,28},{24,16},{28,20},{1,9},{5... | collective-permute-start | bytes 3145736 | tf_op jit(solution)/shard_map/ppermute | solution.py:212
  20.5 24.8 %collective-permute-start.1 = (f32[1,2048]{1,0:T(1,128)S(1)}, f32[1,2048]{1,0:T(1,128)S(1)}, u32[]{:S(2)}, u32[]{:S(2)}) collective-permute-start(f32[1,2048]{1,0:T(1,128)S(1)} %get-tuple-element.20), channel_id=1, source_target_pairs={{0,8},{4,12},{8,0},{12,4},{16,24},{20,28},{24,16},{28,20},{1,9},{5... | collective-permute-start | bytes 24584 | tf_op jit(solution)/shard_map/ppermute | solution.py:213
  46.8 24.8 %collective-permute-start.4 = (bf16[256,2048]{1,0:T(8,128)(2,1)}, bf16[256,2048]{1,0:T(8,128)(2,1)S(1)}, u32[]{:S(2)}, u32[]{:S(2)}) collective-permute-start(bf16[256,2048]{1,0:T(8,128)(2,1)} %add_convert_fusion.1), channel_id=1, source_target_pairs={{0,16},{4,20},{8,24},{12,28},{16,0},{20,4},{24,8},{28,12},{1,17},{... | collective-permute-start | bytes 3145736 | tf_op jit(solution)/shard_map/ppermute | solution.py:212
  48.3 12.4 %copy-start = (f32[32,2,16]{0,2,1:T(8,128)S(1)}, f32[32,2,16]{0,2,1:T(8,128)}, u32[]{:S(2)}) copy-start(f32[32,2,16]{0,2,1:T(8,128)} %param.28) | copy-start | bytes 12292
  61.4 10.1 %collective-permute-start.5 = (f32[1,2048]{1,0:T(1,128)S(1)}, f32[1,2048]{1,0:T(1,128)S(1)}, u32[]{:S(2)}, u32[]{:S(2)}) collective-permute-start(f32[1,2048]{1,0:T(1,128)S(1)} %get-tuple-element.22), channel_id=1, source_target_pairs={{0,16},{4,20},{8,24},{12,28},{16,0},{20,4},{24,8},{28,12},{1,17},{... | collective-permute-start | bytes 24584 | tf_op jit(solution)/shard_map/ppermute | solution.py:213
Sparse Core Ops, SparseCore 0:
  96.2 78.9 reduce-scatter.1

commit v2 on v1

--- a/solution.py
+++ b/solution.py
@@ -204,30 +204,45 @@
 
 def scan_states(state, logs, axis):
     peers, place = (lax.axis_size(axis), lax.axis_index(axis))
-    before = jnp.zeros_like(state)
-    total = state
-    stride = 1
+
+    def swap(value, stride):
+        return lax.ppermute(value, axis, [(p, p ^ stride) for p in range(peers)])
+
+    def join(first, second, second_logs):
+        return jnp.exp(second_logs) * first.astype(F32) + second.astype(F32)
+
+    odd = place % 2 == 1
+    other, other_logs = swap(state, 1), swap(logs, 1)
+    half = state.shape[0] // 2
+
+    def own_half(value):
+        return lax.dynamic_slice_in_dim(value, (place % 2) * half, half, 0)
+
+    mine, theirs = own_half(state), own_half(other)
+    total = join(
+        jnp.where(odd, theirs, mine), jnp.where(odd, mine, theirs), jnp.where(odd, logs, other_logs)
+    ).astype(BF16)
+    total_logs = logs + other_logs
+    before, before_logs = jnp.zeros(total.shape, F32), jnp.zeros_like(logs)
+    stride = 2
     while stride < peers:
-        pairs = [(p, p ^ stride) for p in range(peers)]
-        other = lax.ppermute(total, axis, pairs)
-        other_logs = lax.ppermute(logs, axis, pairs)
         upper = (place // stride) % 2 == 1
-        own_total, own_logs = total, logs
-        first = jnp.where(upper, other, own_total).astype(F32)
-        second = jnp.where(upper, own_total, other).astype(F32)
-        second_logs = jnp.where(upper, own_logs, other_logs)
-        total = (jnp.exp(second_logs) * first + second).astype(BF16)
-        if stride == 1:
-            before_logs = jnp.zeros_like(logs)
-        before = jnp.where(
-            upper,
-            jnp.exp(before_logs) * other.astype(F32) + before.astype(F32),
-            before.astype(F32),
+        far, far_logs = swap(total, stride), swap(total_logs, stride)
+        before = jnp.where(upper, join(far, before, before_logs), before)
+        before_logs = jnp.where(upper, before_logs + far_logs, before_logs)
+        total = join(
+            jnp.where(upper, far, total),
+            jnp.where(upper, total, far),
+            jnp.where(upper, total_logs, far_logs),
         ).astype(BF16)
-        before_logs = jnp.where(upper, before_logs + other_logs, before_logs)
-        logs = own_logs + other_logs
+        total_logs = total_logs + far_logs
         stride *= 2
-    return before, total
+    pack = jnp.stack([before.astype(BF16), total])
+    swapped = swap(pack, 1)
+    low, high = jnp.where(odd, swapped, pack), jnp.where(odd, pack, swapped)
+    both = jnp.concatenate([low, high], axis=1)
+    entered = jnp.where(odd, join(both[0], other, other_logs), both[0].astype(F32))
+    return entered.astype(BF16), both[1]
 
 
 def call(body, outs, scratch=(), flops=0, **more):
@@ -304,7 +319,7 @@
         ],
         out_specs=(block(channels), block(channels)),
     )(prompt_values, prompt_gate, inject, readout, prompt_step, rate, skip)
-    padded = -(-samples // PAD) * PAD
+    padded = -(-samples // (2 * PAD)) * 2 * PAD
     vmem = pl.BlockSpec(memory_space=pltpu.VMEM)
     sample_out, sample_gain, picked = call(
         functools.partial(sample_kernel, dim),
@@ -332,10 +347,176 @@
     return project(normed, out_weight, tokens, samples)
 
 
+def project_kernel(
+    n,
+    normed_ref,
+    weight_ref,
+    out_ref,
+    tiles,
+    sent,
+    from_low,
+    from_high,
+    tile_sems,
+    sent_sems,
+    low_sems,
+    high_sems,
+):
+    place = lax.axis_index("head")
+    chunks, _, width = out_ref.shape
+
+    def tile_copy(d, c):
+        start = (d * chunks + c) * width
+        if not isinstance(start, int):
+            start = pl.multiple_of(start, width)
+        return pltpu.make_async_copy(
+            weight_ref.at[:, pl.ds(start, width)],
+            tiles.at[d, c],
+            tile_sems.at[d, c],
+        )
+
+    for k in range((n + 1) // 2):
+        for c in range(chunks):
+            for d in sorted({n - 1 - k, k}, reverse=True):
+                tile_copy(d, c).start()
+
+    barrier = pltpu.get_barrier_semaphore()
+
+    def greet(to):
+        pl.semaphore_signal(
+            barrier, inc=1, device_id={"head": to}, device_id_type=pl.DeviceIdType.MESH
+        )
+
+    @pl.when(place > 0)
+    def _():
+        greet(place - 1)
+
+    @pl.when(place < n - 1)
+    def _():
+        greet(place + 1)
+
+    inside = (place > 0) & (place < n - 1)
+
+    @pl.when(inside)
+    def _():
+        pl.semaphore_wait(barrier, 2)
+
+    @pl.when(jnp.logical_not(inside))
+    def _():
+        pl.semaphore_wait(barrier, 1)
+
+    def hop(d, c, landing, sems, to):
+        return pltpu.make_async_remote_copy(
+            src_ref=sent.at[d, c],
+            dst_ref=landing.at[d, c],
+            send_sem=sent_sems.at[d, c],
+            recv_sem=sems.at[d, c],
+            device_id={"head": to},
+            device_id_type=pl.DeviceIdType.MESH,
+        )
+
+    def up(d, c):
+        return hop(d, c, from_low, low_sems, place + 1)
+
+    def down(d, c):
+        return hop(d, c, from_high, high_sems, place - 1)
+
+    def share(d, c):
+        tile_copy(d, c).wait()
+        return dot(normed_ref[...], tiles[d, c])
+
+    def pass_on(d, c, move, landing, fed):
+        sent[d, c] = share(d, c).astype(BF16)
+
+        @pl.when(fed)
+        def _():
+            move(d, c).wait_recv()
+            sent[d, c] = (sent[d, c].astype(F32) + landing[d, c].astype(F32)).astype(BF16)
+
+        move(d, c).start()
+
+    def turn(t, carry):
+        k, c = t // chunks, t % chunks
+
+        @pl.when(place < n - 1 - k)
+        def _():
+            pass_on(n - 1 - k, c, up, from_low, place > 0)
+
+        @pl.when(place > k)
+        def _():
+            pass_on(k, c, down, from_high, place < n - 1)
+
+        return carry
+
+    lax.fori_loop(0, (n - 1) * chunks, turn, 0)
+
+    def own(c, carry):
+        out_ref[c] = share(place, c).astype(BF16)
+        return carry
+
+    lax.fori_loop(0, chunks, own, 0)
+
+    def gather(c, carry):
+        @pl.when(place < n - 1)
+        def _():
+            down(place, c).wait_recv()
+            out_ref[c] = (out_ref[c].astype(F32) + from_high[place, c].astype(F32)).astype(BF16)
+
+        @pl.when(place > 0)
+        def _():
+            up(place, c).wait_recv()
+            out_ref[c] = (out_ref[c].astype(F32) + from_low[place, c].astype(F32)).astype(BF16)
+
+        return carry
+
+    lax.fori_loop(0, chunks, gather, 0)
+
+    def drain(t, carry):
+        d, c = t // chunks, t % chunks
+
+        @pl.when(d > place)
+        def _():
+            up(d, c).wait_send()
+
+        @pl.when(d < place)
+        def _():
+            down(d, c).wait_send()
+
+        return carry
+
+    lax.fori_loop(0, n * chunks, drain, 0)
+
+
 def project(normed, out_weight, tokens, samples):
-    share = dot(normed, out_weight).astype(BF16)
-    mixed = lax.psum_scatter(share, "head", scatter_dimension=1, tiled=True)
-    return mixed[:tokens].T, mixed[tokens : tokens + samples].T
+    n = lax.axis_size("head")
+    rows, depth = normed.shape
+    width = 2 * LANES
+    chunks = out_weight.shape[1] // n // width
+    slots = pltpu.VMEM((n, chunks, rows, width), BF16)
+    sems = pltpu.SemaphoreType.DMA((n, chunks))
+    mixed = pl.pallas_call(
+        functools.partial(project_kernel, n),
+        out_shape=jax.ShapeDtypeStruct((chunks, rows, width), BF16),
+        in_specs=[
+            pl.BlockSpec(memory_space=pltpu.VMEM),
+            pl.BlockSpec(memory_space=pl.ANY),
+        ],
+        out_specs=pl.BlockSpec(memory_space=pltpu.VMEM),
+        scratch_shapes=[
+            pltpu.VMEM((n, chunks, depth, width), BF16),
+            slots,
+            slots,
+            slots,
+            sems,
+            sems,
+            sems,
+            sems,
+        ],
+        compiler_params=pltpu.CompilerParams(
+            collective_id=0, has_side_effects=True, vmem_limit_bytes=VMEM_LIMIT
+        ),
+    )(normed, out_weight)
+    mixed = mixed.transpose(0, 2, 1).reshape(chunks * width, rows)
+    return mixed[:, :tokens], mixed[:, tokens : tokens + samples]
 
 
 def solution(mesh):

time: 188 us -> 156 us (0.83)
  waiting for transfers between devices: 110 us -> 23.5 us
  Pallas kernels: 27 us -> 113 us
  matrix products: 14.6 us -> 0 us
  between operations: 14.1 us -> 0.73 us
    pallas_call x0 -> x1, Pallas kernels: none -> 86.5 us  [project(): pl.pallas_call(functools.partial(project_kernel, n), out_shape=jax.ShapeD...]
    reduce_scatter x1 -> x0, waiting for transfers between devices: 79.1 us -> none  [project(): mixed = lax.psum_scatter(share, 'head', scatter_dimension=1, tiled=True)]
    dot_general x1 -> x0, matrix products: 14.6 us -> none  [dot(): lax.dot_general(a, b, (dims, ((), ())), precision=precision, preferred_el...]
    ppermute x6 -> x7, waiting for transfers between devices: 31.2 us -> 23.5 us  [swap(): return lax.ppermute(value, axis, [(p, p ^ stride) for p in range(peers)])]
    convert_element_type x3, other arithmetic: 6.76 us -> 2.88 us  [the longest x1 1.38 us: scan_states(): return (entered.astype(BF16), both[1])]
    transpose x2 -> x0, local copies, waits for them, and re-layouts: 2.61 us -> none  [project(): return (mixed[:tokens].T, mixed[tokens:tokens + samples].T)]
    ppermute x6 -> x7, starting transfers between devices: 4.61 us -> 4.67 us  [swap(): return lax.ppermute(value, axis, [(p, p ^ stride) for p in range(peers)])]
  transfers between devices with their start and end apart: 7 -> 7, of which waited for: 4 -> 3; matrix products, arithmetic and copies ran while one was open for 2% -> 2% of each run, Pallas kernels for 8% -> 9%
where the time goes in v2:
time: 156 us
  Pallas kernels  113 us (72%)
  waiting for transfers between devices  23.5 us (15%)
  other arithmetic  7.14 us (5%)
  local copies, waits for them, and re-layouts  6.35 us (4%)
  starting transfers between devices  4.67 us (3%)
    pallas_call x1, Pallas kernels, project(): pl.pallas_call(functools.partial(project_kernel, n), out_shape=jax.ShapeD...  86.5 us
    ppermute x7, waiting for transfers between devices, swap(): return lax.ppermute(value, axis, [(p, p ^ stride) for p in range(peers)])  23.5 us
    pallas_call x1, Pallas kernels, per_device(): call(functools.partial(local_kernel, dim), (shape((tokens, channels), BF1...  12.2 us
    pallas_call x1, Pallas kernels, per_device(): call(finish_kernel, shape((tokens + padded, channels), BF16), flops=1 << 30)  6.29 us
    pallas_call x1, Pallas kernels, per_device(): call(functools.partial(state_kernel, dim), (shape((entries, channels), BF...  5.87 us
    ppermute x7, starting transfers between devices, swap(): return lax.ppermute(value, axis, [(p, p ^ stride) for p in range(peers)])  4.67 us
  transfers between devices with their start and end apart: 7, of which 3 were waited for; matrix products, arithmetic and copies ran while one was open for 2% of the time, Pallas kernels for 9%

profile of v2, /device:TPU:10, one launch (start us, length us, event | category | flops | bytes accessed | tf_op | source)
XLA Modules:
  0.0 155.8 jit_solution(3913701137022917108)
XLA Ops:
  0.6 0.7 negate_bitcast_fusion
  1.3 0.7 copy.22.rate_ref
  2.0 5.9 %shard_map.158 = (bf16[256,2048]{1,0:T(8,128)(2,1)}, f32[8,2048]{1,0:T(8,128)}) custom-call(bf16[512,2048]{1,0:T(8,128)(2,1)} %values_ref.4, bf16[512,256]{1,0:T(8,128)(2,1)} %bitcast.39, f32[32,512]{1,0:T(8,128)} %step_ref.3, f32[32,1]{1,0:T(8,128)} %copy.22.rate_ref), custom_call_target="tpu_custom_call" | custom-call | flops 2147483648 | bytes 8388608 | tf_op jit(solution)/shard_map/pallas_call | solution.py:288
  7.9 0.0 copy-start.1
  7.9 0.0 copy-start
  7.9 0.0 collective-permute-start.2
  7.9 0.9 slice.16
  8.7 0.5 collective-permute-start
  9.2 1.5 collective-permute-done
  10.7 0.9 slice_add_fusion
  11.6 0.0 collective-permute-done.2
  11.6 1.3 add_convert_fusion.2
  12.9 0.6 collective-permute-start.3
  13.5 1.5 collective-permute-start.1
  15.0 12.1 %collective-permute-done.1 = f32[1,2048]{1,0:T(1,128)S(1)} collective-permute-done((f32[1,2048]{1,0:T(1,128)S(1)}, f32[1,2048]{1,0:T(1,128)S(1)}, u32[]{:S(2)}, u32[]{:S(2)}) %collective-permute-start.1) | collective-permute-done | bytes 8224 | tf_op jit(solution)/shard_map/ppermute | solution.py:209
  27.1 0.0 collective-permute-done.3
  27.1 0.2 add_convert_fusion.1
  27.4 1.6 %collective-permute-start.4 = (bf16[128,2048]{1,0:T(8,128)(2,1)S(1)}, bf16[128,2048]{1,0:T(8,128)(2,1)S(1)}, u32[]{:S(2)}, u32[]{:S(2)}) collective-permute-start(bf16[128,2048]{1,0:T(8,128)(2,1)S(1)} %add_convert_fusion.1), channel_id=1, source_target_pairs={{0,16},{4,20},{8,24},{12,28},{16,0},{20,4},{24,8},{28,12},{1,17},{... | collective-permute-start | bytes 1572872 | tf_op jit(solution)/shard_map/ppermute | solution.py:209
  29.0 0.5 collective-permute-start.5
  29.5 0.0 copy-done.1
  29.5 0.1 broadcast_in_dim.15
  29.5 0.7 broadcast_in_dim_reshape.3.skip_ref
  30.2 0.0 copy-done
  30.2 0.7 copy.24
  30.9 9.8 %collective-permute-done.5 = f32[1,2048]{1,0:T(1,128)S(1)} collective-permute-done((f32[1,2048]{1,0:T(1,128)S(1)}, f32[1,2048]{1,0:T(1,128)S(1)}, u32[]{:S(2)}, u32[]{:S(2)}) %collective-permute-start.5) | collective-permute-done | bytes 8224 | tf_op jit(solution)/shard_map/ppermute | solution.py:209
  40.8 0.0 collective-permute-done.4
  40.8 0.4 fusion.7
  41.2 1.1 pad_maximum_fusion.1
  42.3 0.0 collective-permute-start.6
  42.3 2.5 %shard_map.160 = (f32[16,2048]{1,0:T(8,128)}, f32[16,2048]{1,0:T(8,128)}, f32[16,256]{1,0:T(8,128)}) custom-call(s32[2]{0:T(128)} %length_ref.1, bf16[2,16,2048]{2,1,0:T(8,128)(2,1)} %values_ref.5, bf16[2,16,2048]{2,1,0:T(8,128)(2,1)} %gate_ref.3, bf16[2,16,256]{2,1,0:T(8,128)(2,1)} %bitcast.41, bf16[2,16,256]{2,1,0:T(8,128)(2,1)} %bitcast.42, ...), custom_call_target="tpu_custom_call" | custom-call | flops 4294967296 | bytes 8388608 | tf_op jit(solution)/shard_map/pallas_call | solution.py:324
  44.8 12.2 %shard_map.159 = (bf16[512,2048]{1,0:T(8,128)(2,1)}, bf16[512,2048]{1,0:T(8,128)(2,1)}) custom-call(bf16[512,2048]{1,0:T(8,128)(2,1)} %values_ref.4, bf16[512,2048]{1,0:T(8,128)(2,1)} %gate_ref.2, bf16[512,256]{1,0:T(8,128)(2,1)} %bitcast.40, bf16[512,256]{1,0:T(8,128)(2,1)} %bitcast.30, f32[32,512]{1,0:T(8,128)} %step_ref.3, f32[32,1]{1,0:T(8,128)} %copy.22.rate_ref, ...), custom_call_target="tpu_custom_call" | custom-call | flops 8589934592 | bytes 8388608 | tf_op jit(solution)/shard_map/pallas_call | solution.py:301
  57.1 0.0 collective-permute-done.6
  57.1 0.1 broadcast_select_fusion
  57.2 1.0 fusion.5.final_ref
  58.3 1.4 fusion.1.state_ref
  59.6 6.3 %shard_map.161.normed_ref = bf16[528,2048]{1,0:T(8,128)(2,1)} custom-call(bf16[512,256]{1,0:T(8,128)(2,1)} %bitcast.31, bf16[256,2048]{1,0:T(8,128)(2,1)} %fusion.1.state_ref, bf16[512,2048]{1,0:T(8,128)(2,1)} %get-tuple-element.11.out_ref, bf16[512,2048]{1,0:T(8,128)(2,1)} %get-tuple-element.12.gain_ref, f32[16,256]{1,0:T(8,128)} %get-tuple-element.13.picked_ref, ...), custom_call_target="tpu_custom_call" | custom-call | flops 1073741824 | bytes 8388608 | tf_op jit(solution)/shard_map/pallas_call | solution.py:344
  65.9 86.5 %shard_map.162 = bf16[4,528,256]{2,1,0:T(8,128)(2,1)} custom-call(bf16[528,2048]{1,0:T(8,128)(2,1)} %shard_map.161.normed_ref, bf16[2048,4096]{1,0:T(8,128)(2,1)} %weight_ref.1), custom_call_target="tpu_custom_call" | custom-call | tf_op jit(solution)/shard_map/pallas_call | solution.py:496
  152.4 1.4 copy.28
  153.8 0.6 slice.24
  154.4 0.1 slice.23
  154.5 1.3 copy.27
  (2 shorter events, 0.0 us)
Async XLA Ops:
  7.9 21.6 %copy-start.1 = (f32[32]{0:T(128)S(1)}, f32[32]{0:T(128)}, u32[]{:S(2)}) copy-start(f32[32]{0:T(128)} %param.21) | copy-start | bytes 388
  7.9 22.4 %copy-start = (f32[32,2,16]{0,2,1:T(8,128)S(1)}, f32[32,2,16]{0,2,1:T(8,128)}, u32[]{:S(2)}) copy-start(f32[32,2,16]{0,2,1:T(8,128)} %param.28) | copy-start | bytes 12292
  7.9 3.8 %collective-permute-start.2 = (bf16[256,2048]{1,0:T(8,128)(2,1)}, bf16[256,2048]{1,0:T(8,128)(2,1)S(1)}, u32[]{:S(2)}, u32[]{:S(2)}) collective-permute-start(bf16[256,2048]{1,0:T(8,128)(2,1)} %get-tuple-element.10), channel_id=1, source_target_pairs={{0,4},{4,0},{8,12},{12,8},{16,20},{20,16},{24,28},{28,24},{1,5},{5... | collective-permute-start | bytes 3145736 | tf_op jit(solution)/shard_map/ppermute | solution.py:209
  8.7 2.0 %collective-permute-start = (f32[1,2048]{1,0:T(1,128)S(1)}, f32[1,2048]{1,0:T(1,128)S(1)}, u32[]{:S(2)}, u32[]{:S(2)}) collective-permute-start(f32[1,2048]{1,0:T(1,128)S(1)} %slice.16), channel_id=1, source_target_pairs={{0,4},{4,0},{8,12},{12,8},{16,20},{20,16},{24,28},{28,24},{1,5},{5... | collective-permute-start | bytes 24584 | tf_op jit(solution)/shard_map/ppermute | solution.py:209
  12.9 14.2 %collective-permute-start.3 = (bf16[128,2048]{1,0:T(8,128)(2,1)S(1)}, bf16[128,2048]{1,0:T(8,128)(2,1)S(1)}, u32[]{:S(2)}, u32[]{:S(2)}) collective-permute-start(bf16[128,2048]{1,0:T(8,128)(2,1)S(1)} %add_convert_fusion.2), channel_id=1, source_target_pairs={{0,8},{4,12},{8,0},{12,4},{16,24},{20,28},{24,16},{28,20},{1,9},{5... | collective-permute-start | bytes 1572872 | tf_op jit(solution)/shard_map/ppermute | solution.py:209
  13.5 13.6 %collective-permute-start.1 = (f32[1,2048]{1,0:T(1,128)S(1)}, f32[1,2048]{1,0:T(1,128)S(1)}, u32[]{:S(2)}, u32[]{:S(2)}) collective-permute-start(f32[1,2048]{1,0:T(1,128)S(1)} %get-tuple-element.24), channel_id=1, source_target_pairs={{0,8},{4,12},{8,0},{12,4},{16,24},{20,28},{24,16},{28,20},{1,9},{5... | collective-permute-start | bytes 24584 | tf_op jit(solution)/shard_map/ppermute | solution.py:209
  27.4 13.4 %collective-permute-start.4 = (bf16[128,2048]{1,0:T(8,128)(2,1)S(1)}, bf16[128,2048]{1,0:T(8,128)(2,1)S(1)}, u32[]{:S(2)}, u32[]{:S(2)}) collective-permute-start(bf16[128,2048]{1,0:T(8,128)(2,1)S(1)} %add_convert_fusion.1), channel_id=1, source_target_pairs={{0,16},{4,20},{8,24},{12,28},{16,0},{20,4},{24,8},{28,12},{1,17},{... | collective-permute-start | bytes 1572872 | tf_op jit(solution)/shard_map/ppermute | solution.py:209
  29.0 11.8 %collective-permute-start.5 = (f32[1,2048]{1,0:T(1,128)S(1)}, f32[1,2048]{1,0:T(1,128)S(1)}, u32[]{:S(2)}, u32[]{:S(2)}) collective-permute-start(f32[1,2048]{1,0:T(1,128)S(1)} %get-tuple-element.26), channel_id=1, source_target_pairs={{0,16},{4,20},{8,24},{12,28},{16,0},{20,4},{24,8},{28,12},{1,17},{... | collective-permute-start | bytes 24584 | tf_op jit(solution)/shard_map/ppermute | solution.py:209
  42.3 14.8 %collective-permute-start.6 = (bf16[2,128,2048]{2,1,0:T(8,128)(2,1)}, bf16[2,128,2048]{2,1,0:T(8,128)(2,1)S(1)}, u32[]{:S(2)}, u32[]{:S(2)}) collective-permute-start(bf16[2,128,2048]{2,1,0:T(8,128)(2,1)} %pad_maximum_fusion.1), channel_id=1, source_target_pairs={{0,4},{4,0},{8,12},{12,8},{16,20},{20,16},{24,28},{28,24},{1,5},{5... | collective-permute-start | bytes 3145736 | tf_op jit(solution)/shard_map/ppermute | solution.py:209
